TPU v7x, 128 devices: a whole 4x4x4 slice. The times are simulated.
128 devices in a mesh: ha: 2 (over z_hi), wa: 64 (over y, z_lo, x, core).
Axes of the slice: x: 4, y: 4, z: 4 (z_hi: 2, z_lo: 2; z = z_hi * 2 + z_lo), core: 2. Of those that a mesh axis runs over, the one named last changes fastest.
Arguments:
- queries: float32 [2, 16, 512, 256], P(None, 'ha', 'wa'), may hold values from -240 to 240
- keys: float32 [2, 16, 512, 256], P(None, 'ha', 'wa'), may hold values from -6 to 6
- values: float32 [2, 16, 512, 256], P(None, 'ha', 'wa'), may hold values from -6 to 6
- cotangent: float32 [2, 16, 512, 256], P(None, 'ha', 'wa'), may hold values from -6 to 6
Outputs:
- query_grad: float32 [2, 16, 512, 256], P(None, 'ha', 'wa')
- key_grad: float32 [2, 16, 512, 256], P(None, 'ha', 'wa')
- value_grad: float32 [2, 16, 512, 256], P(None, 'ha', 'wa')
All inputs are finite; a program needn't handle non-finite values.
Results may differ from a plain program's by a relative error of at most 0.0003.
Values sent between devices are 32-bit elements; how exact they have to be, the bound alone decides.
A program may use at most 128 MiB of HBM per device.

v0:
```python
import functools

import jax
import jax.numpy as jnp
from jax import lax
from jax.experimental import pallas as pl
from jax.experimental.pallas import tpu as pltpu
from jax.sharding import PartitionSpec as P

HEADS = 4
REACH = 3
MESH = pl.DeviceIdType.MESH
HIGHEST = lax.Precision.HIGHEST

OWN = 0
LEFT = 64
RIGHT = 88
ROWS = 112
CORNER_LEFT = 136
CORNER_RIGHT = 152
KEYS = 168
BLOCKS = ((LEFT, 24), (RIGHT, 24), (ROWS, 24), (CORNER_LEFT, 16), (CORNER_RIGHT, 16))


def dot(a, b, contract):
    return lax.dot_general(
        a, b, (contract, ((), ())), precision=HIGHEST, preferred_element_type=jnp.float32
    )


def kernel(
    wa_count,
    q_ref,
    k_ref,
    v_ref,
    c_ref,
    dq_ref,
    dk_ref,
    dv_ref,
    wide,
    packed,
    terms,
    back,
    bias,
    qs,
    cs,
    send_sem,
    recv_sem,
    send_sem2,
    recv_sem2,
):
    images, tile_rows, tile_cols, channels = q_ref.shape
    tokens = tile_rows * tile_cols
    head_size = channels // HEADS
    ha = lax.axis_index("ha")
    wa = lax.axis_index("wa")
    other = 1 - ha
    left = lax.rem(wa + wa_count - 1, wa_count)
    right = lax.rem(wa + 1, wa_count)
    owners = ((ha, left), (ha, right), (other, wa), (other, left), (other, right))
    takers = ((ha, right), (ha, left), (other, wa), (other, right), (other, left))

    barrier = pltpu.get_barrier_semaphore()
    for device in owners:
        pl.semaphore_signal(barrier, inc=1, device_id=device, device_id_type=MESH)

    edge = (tile_rows - REACH) * other

    def edge_row(index):
        return pl.multiple_of((edge + index) * tile_cols, tile_cols)

    for image in range(images):
        for field, ref in enumerate((k_ref, v_ref)):
            own = ref[image].reshape(tokens, channels)
            wide[image, field, OWN : OWN + tokens] = own
            for row in range(tile_rows):
                line = own[row * tile_cols : (row + 1) * tile_cols]
                packed[image, 0, field, 3 * row : 3 * row + 3] = line[tile_cols - REACH :]
                packed[image, 1, field, 3 * row : 3 * row + 3] = line[:REACH]
            for row in range(REACH):
                line = wide[image, field, pl.ds(edge_row(row), tile_cols)]
                packed[image, 2, field, 3 * row : 3 * row + 3] = line[tile_cols - REACH :]
                packed[image, 3, field, 3 * row : 3 * row + 3] = line[:REACH]
            for side in (2, 3):
                packed[image, side, field, 9:16] = jnp.zeros((7, channels), jnp.float32)

    pl.semaphore_wait(barrier, len(owners))

    halo = []
    for image in range(images):
        copies = []
        for block, (first, size) in enumerate(BLOCKS):
            if block == 2:
                source = wide.at[image, :, pl.ds(edge_row(0), size)]
            else:
                slot = block if block < 2 else block - 1
                source = packed.at[image, slot, :, pl.ds(0, size)]
            copy = pltpu.make_async_remote_copy(
                src_ref=source,
                dst_ref=wide.at[image, :, pl.ds(first, size)],
                send_sem=send_sem.at[image, block],
                recv_sem=recv_sem.at[image, block],
                device_id=takers[block],
                device_id_type=MESH,
            )
            copy.start()
            copies.append(copy)
        halo.append(copies)

    def coordinates(first, size):
        key = lax.broadcasted_iota(jnp.int32, (size, channels), 0)
        row_base = jnp.where(ha == 0, tile_rows, -REACH)
        third = (key * 11) >> 5
        if first == OWN:
            return key >> 3, key & 7, None
        if first == LEFT:
            return third, key - 3 * third - REACH, wa > 0
        if first == RIGHT:
            return third, key - 3 * third + tile_cols, wa < wa_count - 1
        if first == ROWS:
            return row_base + (key >> 3), key & 7, None
        row = jnp.where(key < 9, row_base + third, 100)
        if first == CORNER_LEFT:
            return row, key - 3 * third - REACH, wa > 0
        return row, key - 3 * third + tile_cols, wa < wa_count - 1

    for first, size in ((OWN, tokens),) + BLOCKS:
        key_row, key_col, live = coordinates(first, size)
        token = lax.broadcasted_iota(jnp.int32, (size, channels), 1) & (tokens - 1)
        row_gap = jnp.abs(key_row - (token >> 3))
        col_gap = jnp.abs(key_col - (token & 7))
        gap = jnp.maximum(row_gap, col_gap)
        if live is not None:
            gap = gap + jnp.where(live, 0, 100)
        bias[first : first + size] = jnp.where(gap <= REACH, 0.0, -1e30)

    lane_head = lax.broadcasted_iota(jnp.int32, (tokens, channels), 1) // head_size
    scale = 1.0 / 8.0
    for image in range(images):
        query = q_ref[image].reshape(tokens, channels) * scale
        cot = c_ref[image].reshape(tokens, channels)
        for head in range(HEADS):
            mine = lane_head == head
            qs[image, head * tokens : (head + 1) * tokens] = jnp.where(mine, query, 0.0)
            cs[image, head * tokens : (head + 1) * tokens] = jnp.where(mine, cot, 0.0)

    returned = []
    for image in range(images):
        for copy in halo[image]:
            copy.wait_recv()
        keys = wide[image, 0]
        values = wide[image, 1]
        scores = dot(keys, qs[image], ((1,), (1,))) + bias[...]
        dprobs = dot(values, cs[image], ((1,), (1,)))
        top = jnp.max(scores, axis=0, keepdims=True)
        expd = jnp.exp(scores - top)
        probs = expd / jnp.sum(expd, axis=0, keepdims=True)
        delta = jnp.sum(probs * dprobs, axis=0, keepdims=True)
        dscores = probs * (dprobs - delta)
        terms[image, 0] = dot(dscores, qs[image], ((1,), (0,)))
        terms[image, 1] = dot(probs, cs[image], ((1,), (0,)))
        copies = []
        for block, (first, size) in enumerate(BLOCKS):
            copy = pltpu.make_async_remote_copy(
                src_ref=terms.at[image, :, pl.ds(first, size)],
                dst_ref=back.at[image, :, pl.ds(first - tokens, size)],
                send_sem=send_sem2.at[image, block],
                recv_sem=recv_sem2.at[image, block],
                device_id=owners[block],
                device_id_type=MESH,
            )
            copy.start()
            copies.append(copy)
        returned.append(copies)
        spread = dot(dscores, keys, ((0,), (0,)))
        total = jnp.zeros((tokens, channels), jnp.float32)
        for head in range(HEADS):
            total = total + jnp.where(
                lane_head == head, spread[head * tokens : (head + 1) * tokens], 0.0
            )
        dq_ref[image] = (total * scale).reshape(tile_rows, tile_cols, channels)
        for field, ref in enumerate((dk_ref, dv_ref)):
            ref[image] = terms[image, field, OWN : OWN + tokens].reshape(
                tile_rows, tile_cols, channels
            )

    high = pl.ds(tile_cols - REACH, REACH)
    low = pl.ds(0, REACH)
    for image in range(images):
        for copy in returned[image]:
            copy.wait_recv()
        for field, ref in enumerate((dk_ref, dv_ref)):
            for row in range(tile_rows):
                ref[image, row, high] += back[image, field, pl.ds(LEFT - tokens + 3 * row, 3)]
                ref[image, row, low] += back[image, field, pl.ds(RIGHT - tokens + 3 * row, 3)]
            for row in range(REACH):
                at = edge + row
                ref[image, at] += back[image, field, pl.ds(ROWS - tokens + 8 * row, 8)]
                ref[image, at, high] += back[
                    image, field, pl.ds(CORNER_LEFT - tokens + 3 * row, 3)
                ]
                ref[image, at, low] += back[
                    image, field, pl.ds(CORNER_RIGHT - tokens + 3 * row, 3)
                ]
    for copies in halo + returned:
        for copy in copies:
            copy.wait_send()


def per_device(wa_count, queries, keys, values, cotangent):
    images, tile_rows, tile_cols, channels = queries.shape
    out = jax.ShapeDtypeStruct(queries.shape, jnp.float32)
    vmem = pl.BlockSpec(memory_space=pltpu.VMEM)
    sems = pltpu.SemaphoreType.DMA((images, len(BLOCKS)))
    return pl.pallas_call(
        functools.partial(kernel, wa_count),
        out_shape=(out, out, out),
        in_specs=[vmem] * 4,
        out_specs=(vmem,) * 3,
        scratch_shapes=[
            pltpu.VMEM((images, 2, KEYS, channels), jnp.float32),
            pltpu.VMEM((images, 4, 2, 24, channels), jnp.float32),
            pltpu.VMEM((images, 2, KEYS, channels), jnp.float32),
            pltpu.VMEM((images, 2, KEYS - 64, channels), jnp.float32),
            pltpu.VMEM((KEYS, channels), jnp.float32),
            pltpu.VMEM((images, 256, channels), jnp.float32),
            pltpu.VMEM((images, 256, channels), jnp.float32),
            sems,
            sems,
            sems,
            sems,
        ],
        compiler_params=pltpu.CompilerParams(collective_id=0, has_side_effects=True),
    )(queries, keys, values, cotangent)


def solution(mesh):
    spec = P(None, "ha", "wa", None)
    return jax.shard_map(
        functools.partial(per_device, mesh.shape["wa"]),
        mesh=mesh,
        in_specs=(spec,) * 4,
        out_specs=(spec,) * 3,
        check_vma=False,
    )
```

profile of v0, /device:TPU:0, one launch (start us, length us, event | category | flops | bytes accessed | tf_op | source)
XLA Modules:
  0.0 29.2 jit_solution(9828138799468351537)
XLA Ops:
  0.6 25.3 %shard_map.67 = (f32[2,8,8,256]{3,2,1,0:T(8,128)}, f32[2,8,8,256]{3,2,1,0:T(8,128)}, f32[2,8,8,256]{3,2,1,0:T(8,128)}) custom-call(f32[2,8,8,256]{3,2,1,0:T(8,128)} %q_ref.1, f32[2,8,8,256]{3,2,1,0:T(8,128)} %k_ref.1, f32[2,8,8,256]{3,2,1,0:T(8,128)} %v_ref.1, f32[2,8,8,256]{3,2,1,0:T(8,128)} %c_ref.1), custom_call_target="tpu_custom_call" | custom-call | tf_op jit(solution)/shard_map/pallas_call | solution.py:215
  25.9 0.0 copy-start.1
  25.9 1.6 %copy.10 = f32[2,8,8,256]{3,2,1,0:T(8,128)} copy(f32[2,8,8,256]{3,2,1,0:T(8,128)} %get-tuple-element.6) | data formatting | bytes 262144
  27.5 0.0 copy-done.1
  27.5 0.0 copy-start
  27.5 0.7 %copy.11 = f32[2,8,8,256]{3,2,1,0:T(8,128)} copy(f32[2,8,8,256]{3,2,1,0:T(8,128)S(1)} %copy-done.1) | data formatting | bytes 262144
  28.2 0.3 %copy-done = f32[2,8,8,256]{3,2,1,0:T(8,128)S(1)} copy-done((f32[2,8,8,256]{3,2,1,0:T(8,128)S(1)}, f32[2,8,8,256]{3,2,1,0:T(8,128)}, u32[]{:S(2)}) %copy-start) | copy-done | bytes 131096
  28.5 0.7 %copy.12 = f32[2,8,8,256]{3,2,1,0:T(8,128)} copy(f32[2,8,8,256]{3,2,1,0:T(8,128)S(1)} %copy-done) | data formatting | bytes 262144
Async XLA Ops:
  25.9 1.6 %copy-start.1 = (f32[2,8,8,256]{3,2,1,0:T(8,128)S(1)}, f32[2,8,8,256]{3,2,1,0:T(8,128)}, u32[]{:S(2)}) copy-start(f32[2,8,8,256]{3,2,1,0:T(8,128)} %get-tuple-element.7) | copy-start | bytes 393220
  27.5 1.0 %copy-start = (f32[2,8,8,256]{3,2,1,0:T(8,128)S(1)}, f32[2,8,8,256]{3,2,1,0:T(8,128)}, u32[]{:S(2)}) copy-start(f32[2,8,8,256]{3,2,1,0:T(8,128)} %get-tuple-element.8) | copy-start | bytes 393220
where the time goes:
time: 29.3 us; the launch traced here: 29.2 us
  Pallas kernels  25.3 us (86%)
  local copies, waits for them, and re-layouts  3.21 us (11%)
  between operations  0.65 us (2%)
    pallas_call x1, Pallas kernels, per_device(): pl.pallas_call(functools.partial(kernel, wa_count), out_shape=(out, out,...  25.3 us
    unnamed x7, local copies, waits for them, and re-layouts  3.21 us

commit v1 on v0

v1 whole, which is shorter than its diff:
```python
import functools

import jax
import jax.numpy as jnp
from jax import lax
from jax.experimental import pallas as pl
from jax.experimental.pallas import tpu as pltpu
from jax.sharding import PartitionSpec as P

HEADS = 4
REACH = 3
MESH = pl.DeviceIdType.MESH
HIGHEST = lax.Precision.HIGHEST

TILE = 8
TOKENS = 64
LEFT = 64
RIGHT = 88
ROWS = 112
CORNER_LEFT = 136
CORNER_RIGHT = 152
WIDE = 168
SLOTS = 32
OUTER = 512
KEY, VALUE, QUERY, COT = range(4)
SCALE = 1.0 / 8.0


def dot(a, b, contract):
    return lax.dot_general(
        a, b, (contract, ((), ())), precision=HIGHEST, preferred_element_type=jnp.float32
    )


def third(index):
    return (index * 11) >> 5


def kernel(
    wa_count,
    q_hbm,
    k_hbm,
    v_hbm,
    c_hbm,
    dq_ref,
    dk_ref,
    dv_ref,
    wide,
    packed,
    corners,
    bias,
    outer_bias,
    pick,
    qs,
    cs,
    outer_q,
    outer_c,
    stats_out,
    stats_in,
    load_sem,
    row_sem,
    col_sem,
    corner_sem,
    stat_sem,
):
    images, tokens, channels = q_hbm.shape
    head_size = channels // HEADS
    ha = lax.axis_index("ha")
    wa = lax.axis_index("wa")
    other = 1 - ha
    has_left = wa > 0
    has_right = wa < wa_count - 1
    left = jnp.maximum(wa - 1, 0)
    right = jnp.minimum(wa + 1, wa_count - 1)

    barrier = pltpu.get_barrier_semaphore()

    def greet(device):
        pl.semaphore_signal(barrier, inc=1, device_id=device, device_id_type=MESH)

    greet((other, wa))

    @pl.when(has_left)
    def _():
        greet((other, left))
        greet((ha, left))

    @pl.when(has_right)
    def _():
        greet((other, right))
        greet((ha, right))

    loads = []
    for field, ref in ((KEY, k_hbm), (VALUE, v_hbm), (QUERY, q_hbm), (COT, c_hbm)):
        load = pltpu.make_async_copy(ref, wide.at[:, field, pl.ds(0, tokens)], load_sem.at[field])
        load.start()
        loads.append(load)

    edge = (TILE - REACH) * other
    row_base = jnp.where(ha == 0, TILE, -REACH)

    def place(first, index):
        part = third(index)
        if first == 0:
            return index >> 3, index & 7, None
        if first == LEFT:
            return part, index - 3 * part - REACH, has_left
        if first == RIGHT:
            return part, index - 3 * part + TILE, has_right
        if first == ROWS:
            return row_base + (index >> 3), index & 7, None
        row = jnp.where(index < 9, row_base + part, 100)
        if first == CORNER_LEFT:
            return row, index - 3 * part - REACH, has_left
        return row, index - 3 * part + TILE, has_right

    def window(key_row, key_col, query_row, query_col, live):
        gap = jnp.maximum(jnp.abs(key_row - query_row), jnp.abs(key_col - query_col))
        if live is not None:
            gap = gap + jnp.where(live, 0, 100)
        return jnp.where(gap <= REACH, 0.0, -1e30)

    def iota(shape, dim):
        return lax.broadcasted_iota(jnp.int32, shape, dim)

    token = iota((1, channels), 1) & (tokens - 1)
    blocks = (
        (0, tokens),
        (LEFT, 24),
        (RIGHT, 24),
        (ROWS, 24),
        (CORNER_LEFT, 16),
        (CORNER_RIGHT, 16),
    )
    for first, size in blocks:
        row, col, live = place(first, iota((size, 1), 0))
        bias[first : first + size] = window(row, col, token >> 3, token & 7, live)
    own = iota((tokens, 1), 0)
    slot = iota((1, 128), 1) & (SLOTS - 1)
    for piece, first in enumerate((LEFT, RIGHT, ROWS)):
        row, col, live = place(first, jnp.minimum(slot, 23))
        row = jnp.where(slot < 24, row, 100)
        outer_bias[:, 128 * piece : 128 * piece + 128] = window(own >> 3, own & 7, row, col, live)
    low_slot = slot < 16
    row_l, col_l, _ = place(CORNER_LEFT, slot & 15)
    row_r, col_r, _ = place(CORNER_RIGHT, slot & 15)
    alive = jnp.where(low_slot, has_left.astype(jnp.int32), has_right.astype(jnp.int32)) > 0
    outer_bias[:, 384:] = window(
        own >> 3, own & 7, jnp.where(low_slot, row_l, row_r), jnp.where(low_slot, col_l, col_r), alive
    )

    part = third(jnp.minimum(slot, 23))
    within = jnp.minimum(slot, 23) - 3 * part
    part_c = third(slot & 15)
    within_c = (slot & 15) - 3 * part_c
    sources = (
        jnp.where(slot < 24, part * TILE + (TILE - REACH) + within, -1000),
        jnp.where(slot < 24, part * TILE + within, -1000),
        jnp.where(slot < 24, edge * TILE + slot, -1000),
        jnp.where(
            (slot & 15) < 9,
            (edge + part_c) * TILE + within_c + jnp.where(low_slot, TILE - REACH, 0),
            -1000,
        ),
    )
    lane_slot_head = iota((1, 128), 1) >> 5
    for piece, source in enumerate(sources):
        lane = source + lane_slot_head * tokens
        pick[:, 128 * piece : 128 * piece + 128] = jnp.where(
            iota((channels, 128), 0) == lane, 1.0, 0.0
        ).astype(jnp.bfloat16)

    def clear(first, size, piece, corner, which):
        for image in range(images):
            for field in range(4):
                wide[image, field, first : first + size] = jnp.zeros((size, channels), jnp.float32)
                wide[image, field, corner : corner + 16] = jnp.zeros((16, channels), jnp.float32)
            stats_in[image, piece] = jnp.zeros((8, 128), jnp.float32)
            stats_in[image, which] = jnp.zeros((8, 128), jnp.float32)

    pl.when(jnp.logical_not(has_left))(lambda: clear(LEFT, 24, 0, CORNER_LEFT, 3))
    pl.when(jnp.logical_not(has_right))(lambda: clear(RIGHT, 24, 1, CORNER_RIGHT, 4))

    for field in range(4):
        loads[field].wait()
        for image in range(images):
            mine = wide[image, field, 0:tokens]
            for row in range(TILE):
                line = mine[row * TILE : (row + 1) * TILE]
                packed[image, 0, field, 3 * row : 3 * row + 3] = line[TILE - REACH :]
                packed[image, 1, field, 3 * row : 3 * row + 3] = line[:REACH]

    pl.semaphore_wait(
        barrier, 1 + 2 * has_left.astype(jnp.int32) + 2 * has_right.astype(jnp.int32)
    )

    def remote(source, target, sems, index, device):
        return pltpu.make_async_remote_copy(
            src_ref=source,
            dst_ref=target,
            send_sem=sems.at[(0,) + index],
            recv_sem=sems.at[(1,) + index],
            device_id=device,
            device_id_type=MESH,
        )

    edge_start = pl.multiple_of(edge * TILE, TILE)
    pairs = ((KEY, 2), (QUERY, 2))

    def rows_copy(image, pair):
        fields = pl.ds(*pairs[pair])
        return remote(
            wide.at[image, fields, pl.ds(edge_start, 24)],
            wide.at[image, fields, pl.ds(ROWS, 24)],
            row_sem,
            (image, pair),
            (other, wa),
        )

    targets = ((ha, right), (ha, left))
    senders = (has_left, has_right)
    sends = (has_right, has_left)

    def cols_copy(image, pair, side):
        fields = pl.ds(*pairs[pair])
        return remote(
            packed.at[image, side, fields],
            wide.at[image, fields, pl.ds((LEFT, RIGHT)[side], 24)],
            col_sem,
            (image, pair, side),
            targets[side],
        )

    def corner_copy(image, pair, side):
        fields = pl.ds(*pairs[pair])
        return remote(
            corners.at[image, side, fields],
            wide.at[image, fields, pl.ds((CORNER_LEFT, CORNER_RIGHT)[side], 16)],
            corner_sem,
            (image, pair, side),
            targets[side],
        )

    stat_targets = (
        (ha, right),
        (ha, left),
        (other, wa),
        (other, right),
        (other, left),
    )
    stat_sends = (has_right, has_left, None, has_right, has_left)
    stat_arrives = (has_left, has_right, None, has_left, has_right)

    def stat_copy(image, piece):
        return remote(
            stats_out.at[image, min(piece, 3)],
            stats_in.at[image, piece],
            stat_sem,
            (image, piece),
            stat_targets[piece],
        )

    def if_(condition, action):
        if condition is None:
            action()
        else:
            pl.when(condition)(action)

    for pair in range(2):
        for image in range(images):
            rows_copy(image, pair).start()
        for image in range(images):
            for side in range(2):
                if_(sends[side], cols_copy(image, pair, side).start)

    lane_head = iota((tokens, channels), 1) // head_size
    for image in range(images):
        query = wide[image, QUERY, 0:tokens] * SCALE
        cot = wide[image, COT, 0:tokens]
        for head in range(HEADS):
            mine = lane_head == head
            qs[image, head * tokens : (head + 1) * tokens] = jnp.where(mine, query, 0.0)
            cs[image, head * tokens : (head + 1) * tokens] = jnp.where(mine, cot, 0.0)

    def forward(image, pair):
        rows_copy(image, pair).wait_recv()
        for field in range(2 * pair, 2 * pair + 2):
            for row in range(REACH):
                line = wide[image, field, ROWS + TILE * row : ROWS + TILE * (row + 1)]
                corners[image, 0, field, 3 * row : 3 * row + 3] = line[TILE - REACH :]
                corners[image, 1, field, 3 * row : 3 * row + 3] = line[:REACH]
            for side in range(2):
                corners[image, side, field, 9:16] = jnp.zeros((7, channels), jnp.float32)
        for side in range(2):
            if_(sends[side], corner_copy(image, pair, side).start)

    def arrived(image, pair):
        for side in range(2):
            if_(senders[side], cols_copy(image, pair, side).wait_recv)
        for side in range(2):
            if_(senders[side], corner_copy(image, pair, side).wait_recv)

    def inner(image):
        keys = wide[image, KEY]
        scores = dot(keys, qs[image], ((1,), (1,))) + bias[...]
        dprobs = dot(wide[image, VALUE], cs[image], ((1,), (1,)))
        top = jnp.max(scores, axis=0, keepdims=True)
        expd = jnp.exp(scores - top)
        norm = 1.0 / jnp.sum(expd, axis=0, keepdims=True)
        probs = expd * norm
        delta = jnp.sum(probs * dprobs, axis=0, keepdims=True)
        dscores = probs * (dprobs - delta)

        sheet = jnp.concatenate([top, norm, delta, jnp.zeros((5, channels), jnp.float32)], axis=0)
        high = sheet.astype(jnp.bfloat16)
        rest = sheet - high.astype(jnp.float32)
        middle = rest.astype(jnp.bfloat16)
        low = (rest - middle.astype(jnp.float32)).astype(jnp.bfloat16)
        picked = [
            lax.dot_general(
                term, pick[...], (((1,), (0,)), ((), ())), preferred_element_type=jnp.float32
            )
            for term in (high, middle, low)
        ]
        moved = picked[0] + picked[1] + picked[2]
        for piece in range(4):
            stats_out[image, piece] = moved[:, 128 * piece : 128 * piece + 128]
        for piece in range(5):
            if_(stat_sends[piece], stat_copy(image, piece).start)

        spread = dot(dscores, keys, ((0,), (0,)))
        total = jnp.zeros((tokens, channels), jnp.float32)
        for head in range(HEADS):
            total = total + jnp.where(
                lane_head == head, spread[head * tokens : (head + 1) * tokens], 0.0
            )
        dq_ref[image] = total * SCALE
        dk_ref[image] = dot(dscores[:tokens], qs[image], ((1,), (0,)))
        dv_ref[image] = dot(probs[:tokens], cs[image], ((1,), (0,)))

    def outer(image):
        for field, stack, factor in ((QUERY, outer_q, SCALE), (COT, outer_c, 1.0)):
            for piece, first in enumerate((LEFT, RIGHT, ROWS)):
                block = wide[image, field, first : first + 24] * factor
                for head in range(HEADS):
                    base = 128 * piece + SLOTS * head
                    stack[base : base + 24] = jnp.where(lane_head[:24] == head, block, 0.0)
                    stack[base + 24 : base + 32] = jnp.zeros((8, channels), jnp.float32)
            for half, first in enumerate((CORNER_LEFT, CORNER_RIGHT)):
                block = wide[image, field, first : first + 16] * factor
                for head in range(HEADS):
                    base = 384 + SLOTS * head + 16 * half
                    stack[base : base + 16] = jnp.where(lane_head[:16] == head, block, 0.0)
        scores = dot(wide[image, KEY, 0:tokens], outer_q[...], ((1,), (1,))) + outer_bias[...]
        dprobs = dot(wide[image, VALUE, 0:tokens], outer_c[...], ((1,), (1,)))
        for piece in range(5):
            if_(stat_arrives[piece], stat_copy(image, piece).wait_recv)
        sheet = jnp.concatenate(
            [stats_in[image, 0], stats_in[image, 1], stats_in[image, 2]]
            + [jnp.where(low_slot, stats_in[image, 3], stats_in[image, 4])],
            axis=1,
        )
        probs = jnp.exp(scores - sheet[0:1]) * sheet[1:2]
        dscores = probs * (dprobs - sheet[2:3])
        dk_ref[image] += dot(dscores, outer_q[...], ((1,), (0,)))
        dv_ref[image] += dot(probs, outer_c[...], ((1,), (0,)))

    for image in range(images):
        forward(image, 0)
    arrived(0, 0)
    inner(0)
    for image in range(images):
        forward(image, 1)
    arrived(1, 0)
    inner(1)
    for image in range(images):
        arrived(image, 1)
        outer(image)

    for image in range(images):
        for pair in range(2):
            rows_copy(image, pair).wait_send()
            for side in range(2):
                if_(sends[side], cols_copy(image, pair, side).wait_send)
                if_(sends[side], corner_copy(image, pair, side).wait_send)
        for piece in range(5):
            if_(stat_sends[piece], stat_copy(image, piece).wait_send)


def per_device(wa_count, queries, keys, values, cotangent):
    images, tile_rows, tile_cols, channels = queries.shape
    flat = (images, tile_rows * tile_cols, channels)
    f32 = jnp.float32
    out = jax.ShapeDtypeStruct(flat, f32)
    sems = pltpu.SemaphoreType.DMA
    results = pl.pallas_call(
        functools.partial(kernel, wa_count),
        out_shape=(out, out, out),
        in_specs=[pl.BlockSpec(memory_space=pl.ANY)] * 4,
        out_specs=(pl.BlockSpec(memory_space=pltpu.VMEM),) * 3,
        scratch_shapes=[
            pltpu.VMEM((images, 4, WIDE, channels), f32),
            pltpu.VMEM((images, 2, 4, 24, channels), f32),
            pltpu.VMEM((images, 2, 4, 16, channels), f32),
            pltpu.VMEM((WIDE, channels), f32),
            pltpu.VMEM((TOKENS, OUTER), f32),
            pltpu.VMEM((channels, OUTER), jnp.bfloat16),
            pltpu.VMEM((images, HEADS * TOKENS, channels), f32),
            pltpu.VMEM((images, HEADS * TOKENS, channels), f32),
            pltpu.VMEM((OUTER, channels), f32),
            pltpu.VMEM((OUTER, channels), f32),
            pltpu.VMEM((images, 4, 8, 128), f32),
            pltpu.VMEM((images, 5, 8, 128), f32),
            sems((4,)),
            sems((2, images, 2)),
            sems((2, images, 2, 2)),
            sems((2, images, 2, 2)),
            sems((2, images, 5)),
        ],
        compiler_params=pltpu.CompilerParams(collective_id=0, has_side_effects=True),
    )(*(x.reshape(flat) for x in (queries, keys, values, cotangent)))
    return tuple(x.reshape(queries.shape) for x in results)


def solution(mesh):
    spec = P(None, "ha", "wa", None)
    return jax.shard_map(
        functools.partial(per_device, mesh.shape["wa"]),
        mesh=mesh,
        in_specs=(spec,) * 4,
        out_specs=(spec,) * 3,
        check_vma=False,
    )
```

time: 29.3 us -> 30.9 us (1.055)
  the two profiles are of different devices: /device:TPU:0 before, /device:TPU:24 now
where the time goes in v1:
time: 30.9 us; the launch traced here: 30.8 us
  Pallas kernels  26.9 us (87%)
  local copies, waits for them, and re-layouts  3.21 us (10%)
  between operations  0.65 us (2%)
    pallas_call x1, Pallas kernels, per_device(): pl.pallas_call(functools.partial(kernel, wa_count), out_shape=(out, out,...  26.9 us
    unnamed x7, local copies, waits for them, and re-layouts  3.21 us

profile of v1, /device:TPU:24, one launch (start us, length us, event | category | flops | bytes accessed | tf_op | source)
XLA Modules:
  0.0 30.8 jit_solution(11094941215236943690)
XLA Ops:
  0.6 26.9 %shard_map.67 = (f32[2,64,256]{2,1,0:T(8,128)}, f32[2,64,256]{2,1,0:T(8,128)}, f32[2,64,256]{2,1,0:T(8,128)}) custom-call(f32[2,64,256]{2,1,0:T(8,128)} %bitcast.10, f32[2,64,256]{2,1,0:T(8,128)} %bitcast.11, f32[2,64,256]{2,1,0:T(8,128)} %bitcast.12, f32[2,64,256]{2,1,0:T(8,128)} %bitcast.13), custom_call_target="tpu_custom_call" | custom-call | tf_op jit(solution)/shard_map/pallas_call | solution.py:396
  27.5 0.0 copy-start.1
  27.6 1.6 %copy.10 = f32[2,8,8,256]{3,2,1,0:T(8,128)} copy(f32[2,8,8,256]{3,2,1,0:T(8,128)} %bitcast.9) | data formatting | bytes 262144
  29.2 0.0 copy-done.1
  29.2 0.0 copy-start
  29.2 0.7 %copy.11 = f32[2,8,8,256]{3,2,1,0:T(8,128)} copy(f32[2,8,8,256]{3,2,1,0:T(8,128)S(1)} %bitcast.8) | data formatting | bytes 262144
  29.8 0.3 copy-done
  30.1 0.7 %copy.12 = f32[2,8,8,256]{3,2,1,0:T(8,128)} copy(f32[2,8,8,256]{3,2,1,0:T(8,128)S(1)} %bitcast.7) | data formatting | bytes 262144
Async XLA Ops:
  27.5 1.6 %copy-start.1 = (f32[2,64,256]{2,1,0:T(8,128)S(1)}, f32[2,64,256]{2,1,0:T(8,128)}, u32[]{:S(2)}) copy-start(f32[2,64,256]{2,1,0:T(8,128)} %get-tuple-element.7) | copy-start | bytes 393220
  29.2 1.0 %copy-start = (f32[2,64,256]{2,1,0:T(8,128)S(1)}, f32[2,64,256]{2,1,0:T(8,128)}, u32[]{:S(2)}) copy-start(f32[2,64,256]{2,1,0:T(8,128)} %get-tuple-element.8) | copy-start | bytes 393220

commit v2 on v1

v2 whole, which is shorter than its diff:
```python
import functools

import jax
import jax.numpy as jnp
from jax import lax
from jax.experimental import pallas as pl
from jax.experimental.pallas import tpu as pltpu
from jax.sharding import PartitionSpec as P

HEADS = 4
REACH = 3
MESH = pl.DeviceIdType.MESH

TILE = 8
TOKENS = 64
LEFT = 64
RIGHT = 88
ROWS = 112
CORNER_LEFT = 136
CORNER_RIGHT = 152
FULL = 168
WIDE = 176
OUTER = WIDE - TOKENS
KEY, VALUE, QUERY, COT = range(4)
SCALE = 1.0 / 8.0


def dot(a, b, contract):
    return lax.dot_general(a, b, (contract, ((), ())), preferred_element_type=jnp.float32)


def split(x, parts):
    out = []
    for index in range(parts):
        part = x.astype(jnp.bfloat16)
        out.append(part)
        if index + 1 < parts:
            x = x - part.astype(jnp.float32)
    return out


def beside(parts, order):
    return jnp.concatenate([parts[index] for index in order], axis=1)


def below(parts, order):
    return jnp.concatenate([parts[index] for index in order], axis=0)


def product(a, b, order, contract):
    left = beside if contract[0][0] else below
    right = beside if contract[1][0] else below
    return dot(left(a, [i for i, _ in order]), right(b, [j for _, j in order]), contract)


SIX = ((2, 0), (0, 2), (1, 1), (1, 0), (0, 1), (0, 0))
THREE = ((1, 0), (0, 1), (0, 0))


def third(index):
    return (index * 11) >> 5


def kernel(
    wa_count,
    q_hbm,
    k_hbm,
    v_hbm,
    c_hbm,
    dq_ref,
    dk_ref,
    dv_ref,
    wide,
    packed,
    corners,
    bias,
    outer_bias,
    chosen,
    same_head,
    qs,
    cs,
    ks,
    vs,
    stats_out,
    stats_in,
    load_sem,
    row_sem,
    col_sem,
    corner_sem,
    stat_sem,
):
    images, tokens, channels = q_hbm.shape
    head_size = channels // HEADS
    ha = lax.axis_index("ha")
    wa = lax.axis_index("wa")
    other = 1 - ha
    has_left = wa > 0
    has_right = wa < wa_count - 1
    left = jnp.maximum(wa - 1, 0)
    right = jnp.minimum(wa + 1, wa_count - 1)

    barrier = pltpu.get_barrier_semaphore()

    def greet(device):
        pl.semaphore_signal(barrier, inc=1, device_id=device, device_id_type=MESH)

    greet((other, wa))

    @pl.when(has_left)
    def _():
        greet((other, left))
        greet((ha, left))

    @pl.when(has_right)
    def _():
        greet((other, right))
        greet((ha, right))

    loads = []
    for field, ref in ((KEY, k_hbm), (VALUE, v_hbm), (QUERY, q_hbm), (COT, c_hbm)):
        load = pltpu.make_async_copy(ref, wide.at[:, field, pl.ds(0, tokens)], load_sem.at[field])
        load.start()
        loads.append(load)

    edge = (TILE - REACH) * other
    row_base = jnp.where(ha == 0, TILE, -REACH)

    def place(first, index):
        part = third(index)
        if first == 0:
            return index >> 3, index & 7, None
        if first == LEFT:
            return part, index - 3 * part - REACH, has_left
        if first == RIGHT:
            return part, index - 3 * part + TILE, has_right
        if first == ROWS:
            return row_base + (index >> 3), index & 7, None
        row = jnp.where(index < 9, row_base + part, 100)
        if first == CORNER_LEFT:
            return row, index - 3 * part - REACH, has_left
        return row, index - 3 * part + TILE, has_right

    def window(key_row, key_col, query_row, query_col, live):
        gap = jnp.maximum(jnp.abs(key_row - query_row), jnp.abs(key_col - query_col))
        if live is not None:
            gap = gap + jnp.where(live, 0, 100)
        return jnp.where(gap <= REACH, 0.0, -1e30)

    def iota(shape, dim):
        return lax.broadcasted_iota(jnp.int32, shape, dim)

    token = iota((1, channels), 1) & (tokens - 1)
    blocks = (
        (0, tokens),
        (LEFT, 24),
        (RIGHT, 24),
        (ROWS, 24),
        (CORNER_LEFT, 16),
        (CORNER_RIGHT, 16),
    )
    lane_token = iota((1, channels), 1) & (tokens - 1)
    for first, size in blocks:
        row, col, live = place(first, iota((size, 1), 0))
        bias[first : first + size] = window(row, col, token >> 3, token & 7, live)
        if first:
            low = first - tokens
            outer_bias[low : low + size] = window(
                lane_token >> 3, lane_token & 7, row, col, live
            )
            col = (col + TILE) & 7
            row = jnp.where(row < 0, row + TILE, row) & 7 if first >= ROWS else row
            chosen[low : low + size] = jnp.where(lane_token == row * TILE + col, 1.0, 0.0)
    bias[FULL:WIDE] = jnp.full((WIDE - FULL, channels), -1e30, jnp.float32)
    outer_bias[FULL - tokens :] = jnp.full((WIDE - FULL, channels), -1e30, jnp.float32)
    chosen[FULL - tokens :] = jnp.zeros((WIDE - FULL, channels), jnp.float32)
    same_head[...] = jnp.where(
        (iota((channels, channels), 0) >> 6) == (iota((channels, channels), 1) >> 6), 1.0, 0.0
    ).astype(jnp.bfloat16)
    for image in range(images):
        for field in range(4):
            wide[image, field, FULL:WIDE] = jnp.zeros((WIDE - FULL, channels), jnp.float32)

    def clear(first, size, piece, corner, which):
        for image in range(images):
            for field in range(4):
                wide[image, field, first : first + size] = jnp.zeros((size, channels), jnp.float32)
                wide[image, field, corner : corner + 16] = jnp.zeros((16, channels), jnp.float32)
            stats_in[image, piece] = jnp.zeros((8, channels), jnp.float32)
            stats_in[image, which] = jnp.zeros((8, channels), jnp.float32)

    pl.when(jnp.logical_not(has_left))(lambda: clear(LEFT, 24, 0, CORNER_LEFT, 3))
    pl.when(jnp.logical_not(has_right))(lambda: clear(RIGHT, 24, 1, CORNER_RIGHT, 4))

    def pack(pair):
        for field in range(2 * pair, 2 * pair + 2):
            loads[field].wait()
            for image in range(images):
                mine = wide[image, field, 0:tokens]
                for row in range(TILE):
                    line = mine[row * TILE : (row + 1) * TILE]
                    packed[image, 0, field, 3 * row : 3 * row + 3] = line[TILE - REACH :]
                    packed[image, 1, field, 3 * row : 3 * row + 3] = line[:REACH]

    pack(0)
    pl.semaphore_wait(
        barrier, 1 + 2 * has_left.astype(jnp.int32) + 2 * has_right.astype(jnp.int32)
    )

    def remote(source, target, sems, index, device):
        return pltpu.make_async_remote_copy(
            src_ref=source,
            dst_ref=target,
            send_sem=sems.at[(0,) + index],
            recv_sem=sems.at[(1,) + index],
            device_id=device,
            device_id_type=MESH,
        )

    edge_start = pl.multiple_of(edge * TILE, TILE)
    pairs = ((KEY, 2), (QUERY, 2))

    def rows_copy(image, pair):
        fields = pl.ds(*pairs[pair])
        return remote(
            wide.at[image, fields, pl.ds(edge_start, 24)],
            wide.at[image, fields, pl.ds(ROWS, 24)],
            row_sem,
            (image, pair),
            (other, wa),
        )

    targets = ((ha, right), (ha, left))
    senders = (has_left, has_right)
    sends = (has_right, has_left)

    def cols_copy(image, pair, side):
        fields = pl.ds(*pairs[pair])
        return remote(
            packed.at[image, side, fields],
            wide.at[image, fields, pl.ds((LEFT, RIGHT)[side], 24)],
            col_sem,
            (image, pair, side),
            targets[side],
        )

    def corner_copy(image, pair, side):
        fields = pl.ds(*pairs[pair])
        return remote(
            corners.at[image, side, fields],
            wide.at[image, fields, pl.ds((CORNER_LEFT, CORNER_RIGHT)[side], 16)],
            corner_sem,
            (image, pair, side),
            targets[side],
        )

    stat_targets = (
        (ha, right),
        (ha, left),
        (other, wa),
        (other, right),
        (other, left),
    )
    stat_sends = (has_right, has_left, None, has_right, has_left)
    stat_arrives = (has_left, has_right, None, has_left, has_right)

    def stat_copy(image, piece):
        return remote(
            stats_out.at[image],
            stats_in.at[image, piece],
            stat_sem,
            (image, piece),
            stat_targets[piece],
        )

    def if_(condition, action):
        if condition is None:
            action()
        else:
            pl.when(condition)(action)

    for pair in range(2):
        if pair:
            pack(pair)
        for image in range(images):
            rows_copy(image, pair).start()
        for image in range(images):
            for side in range(2):
                if_(sends[side], cols_copy(image, pair, side).start)

    lane_head = iota((tokens, channels), 1) // head_size
    heads = [jnp.where(lane_head == head, 1.0, 0.0).astype(jnp.bfloat16) for head in range(HEADS)]
    for image in range(images):
        for field, stack, factor, parts in (
            (QUERY, qs, SCALE, 3),
            (COT, cs, 1.0, 2),
            (KEY, ks, 1.0, 3),
            (VALUE, vs, 1.0, 2),
        ):
            for index, part in enumerate(split(wide[image, field, 0:tokens] * factor, parts)):
                for head in range(HEADS):
                    stack[image, index, head * tokens : (head + 1) * tokens] = part * heads[head]

    def forward(image, pair):
        rows_copy(image, pair).wait_recv()
        for field in range(2 * pair, 2 * pair + 2):
            for row in range(REACH):
                line = wide[image, field, ROWS + TILE * row : ROWS + TILE * (row + 1)]
                corners[image, 0, field, 3 * row : 3 * row + 3] = line[TILE - REACH :]
                corners[image, 1, field, 3 * row : 3 * row + 3] = line[:REACH]
            for side in range(2):
                corners[image, side, field, 9:16] = jnp.zeros((7, channels), jnp.float32)
        for side in range(2):
            if_(sends[side], corner_copy(image, pair, side).start)

    def arrived(image, pair):
        for side in range(2):
            if_(senders[side], cols_copy(image, pair, side).wait_recv)
        for side in range(2):
            if_(senders[side], corner_copy(image, pair, side).wait_recv)

    def parts_of(ref, image, count):
        return [ref[image, index] for index in range(count)]

    def fold(stacked):
        total = jnp.zeros((tokens, channels), jnp.float32)
        for head in range(HEADS):
            total = total + jnp.where(
                lane_head == head, stacked[head * tokens : (head + 1) * tokens], 0.0
            )
        return total

    def statistics(image):
        keys = split(wide[image, KEY], 3)
        scores = product(keys, parts_of(qs, image, 3), SIX, ((1,), (1,))) + bias[...]
        values = split(wide[image, VALUE], 2)
        dprobs = product(values, parts_of(cs, image, 2), THREE, ((1,), (1,)))
        top = jnp.max(scores, axis=0, keepdims=True)
        expd = jnp.exp(scores - top)
        norm = 1.0 / jnp.sum(expd, axis=0, keepdims=True)
        probs = expd * norm
        delta = jnp.sum(probs * dprobs, axis=0, keepdims=True)
        stats_out[image, 0:1] = top
        stats_out[image, 1:2] = norm
        stats_out[image, 2:3] = delta
        stats_out[image, 3:8] = jnp.zeros((5, channels), jnp.float32)
        for piece in range(5):
            if_(stat_sends[piece], stat_copy(image, piece).start)
        return keys, probs, probs * (dprobs - delta)

    def inner(image, keys, probs, dscores):
        dparts = split(dscores, 2)
        dq_ref[image] = fold(product(dparts, keys, THREE, ((0,), (0,)))) * SCALE
        own = [part[:tokens] for part in dparts]
        dk_ref[image] = product(own, parts_of(qs, image, 2), THREE, ((1,), (0,)))
        own = split(probs[:tokens], 2)
        dv_ref[image] = product(own, parts_of(cs, image, 2), THREE, ((1,), (0,)))

    def outer(image):
        queries = split(wide[image, QUERY, tokens:WIDE] * SCALE, 3)
        cots = split(wide[image, COT, tokens:WIDE], 2)
        scores = product(queries, parts_of(ks, image, 3), SIX, ((1,), (1,))) + outer_bias[...]
        dprobs = product(cots, parts_of(vs, image, 2), THREE, ((1,), (1,)))
        return queries, cots, scores, dprobs

    def finish(image, queries, cots, scores, dprobs):
        for piece in range(5):
            if_(stat_arrives[piece], stat_copy(image, piece).wait_recv)
        spread = []
        for which in range(3):
            lines = [
                chosen[first - tokens : first - tokens + size] * stats_in[image, piece, which : which + 1]
                for piece, (first, size) in enumerate(blocks[1:])
            ]
            spread.append(jnp.concatenate(lines + [jnp.zeros((WIDE - FULL, channels), jnp.float32)], 0))
        terms = split(jnp.concatenate(spread, 0), 3)
        table = same_head[...]
        sheet = dot(beside(terms, (2, 1, 0)), below([table], (0, 0, 0)), ((1,), (0,)))
        top, norm, delta = (sheet[OUTER * index : OUTER * (index + 1)] for index in range(3))
        probs = jnp.exp(scores - top) * norm
        dscores = probs * (dprobs - delta)
        dk_ref[image] += fold(product(split(dscores, 2), queries, THREE, ((0,), (0,))))
        dv_ref[image] += fold(product(split(probs, 2), cots, THREE, ((0,), (0,))))

    for image in range(images):
        forward(image, 0)
    kept = []
    for image in range(images):
        arrived(image, 0)
        kept.append(statistics(image))
    for image in range(images):
        forward(image, 1)
    for image in range(images):
        inner(image, *kept[image])
    kept = []
    for image in range(images):
        arrived(image, 1)
        kept.append(outer(image))
    for image in range(images):
        finish(image, *kept[image])

    for image in range(images):
        for pair in range(2):
            rows_copy(image, pair).wait_send()
            for side in range(2):
                if_(sends[side], cols_copy(image, pair, side).wait_send)
                if_(sends[side], corner_copy(image, pair, side).wait_send)
        for piece in range(5):
            if_(stat_sends[piece], stat_copy(image, piece).wait_send)


def store(*refs):
    sem = refs[6]
    copies = [pltpu.make_async_copy(refs[i], refs[3 + i], sem.at[i]) for i in range(3)]
    for copy in copies:
        copy.start()
    for copy in copies:
        copy.wait()


def per_device(wa_count, queries, keys, values, cotangent):
    images, tile_rows, tile_cols, channels = queries.shape
    flat = (images, tile_rows * tile_cols, channels)
    f32 = jnp.float32
    out = jax.ShapeDtypeStruct(flat, f32)
    sems = pltpu.SemaphoreType.DMA
    results = pl.pallas_call(
        functools.partial(kernel, wa_count),
        out_shape=(pltpu.VMEM(flat, f32),) * 3,
        in_specs=[pl.BlockSpec(memory_space=pl.ANY)] * 4,
        out_specs=(pl.BlockSpec(memory_space=pltpu.VMEM),) * 3,
        scratch_shapes=[
            pltpu.VMEM((images, 4, WIDE, channels), f32),
            pltpu.VMEM((images, 2, 4, 24, channels), f32),
            pltpu.VMEM((images, 2, 4, 16, channels), f32),
            pltpu.VMEM((WIDE, channels), f32),
            pltpu.VMEM((OUTER, channels), f32),
            pltpu.VMEM((OUTER, channels), f32),
            pltpu.VMEM((channels, channels), jnp.bfloat16),
            pltpu.VMEM((images, 3, HEADS * TOKENS, channels), jnp.bfloat16),
            pltpu.VMEM((images, 2, HEADS * TOKENS, channels), jnp.bfloat16),
            pltpu.VMEM((images, 3, HEADS * TOKENS, channels), jnp.bfloat16),
            pltpu.VMEM((images, 2, HEADS * TOKENS, channels), jnp.bfloat16),
            pltpu.VMEM((images, 8, channels), f32),
            pltpu.VMEM((images, 5, 8, channels), f32),
            sems((4,)),
            sems((2, images, 2)),
            sems((2, images, 2, 2)),
            sems((2, images, 2, 2)),
            sems((2, images, 5)),
        ],
        compiler_params=pltpu.CompilerParams(collective_id=0, has_side_effects=True),
    )(*(x.reshape(flat) for x in (queries, keys, values, cotangent)))
    results = pl.pallas_call(
        store,
        out_shape=(out, out, out),
        in_specs=[pl.BlockSpec(memory_space=pltpu.VMEM)] * 3,
        out_specs=(pl.BlockSpec(memory_space=pl.ANY),) * 3,
        scratch_shapes=[sems((3,))],
    )(*(pltpu.with_memory_space_constraint(x, pltpu.VMEM) for x in results))
    return tuple(x.reshape(queries.shape) for x in results)


def solution(mesh):
    spec = P(None, "ha", "wa", None)
    return jax.shard_map(
        functools.partial(per_device, mesh.shape["wa"]),
        mesh=mesh,
        in_specs=(spec,) * 4,
        out_specs=(spec,) * 3,
        check_vma=False,
    )
```

time: 30.9 us -> 26 us (0.84)
  local copies, waits for them, and re-layouts: 3.21 us -> 0 us
  Pallas kernels: 26.9 us -> 25.2 us
    unnamed x7 -> x0, local copies, waits for them, and re-layouts: 3.21 us -> none
    pallas_call x1 -> x2, Pallas kernels: 26.9 us -> 25.2 us  [the longest x1 24.5 us: per_device(): pl.pallas_call(functools.partial(kernel, wa_count), out_shape=(pltpu.VMEM...]
where the time goes in v2:
time: 26 us; the launch traced here: 25.9 us
  Pallas kernels  25.2 us (97%)
  between operations  0.64 us (2%)
    pallas_call x1, Pallas kernels, per_device(): pl.pallas_call(functools.partial(kernel, wa_count), out_shape=(pltpu.VMEM...  24.5 us
    pallas_call x1, Pallas kernels, per_device(): pl.pallas_call(store, out_shape=(out, out, out), in_specs=[pl.BlockSpec(m...  0.77 us

profile of v2, /device:TPU:24, one launch (start us, length us, event | category | flops | bytes accessed | tf_op | source)
XLA Modules:
  0.0 25.9 jit_solution(4586244283126873027)
XLA Ops:
  0.6 24.5 %shard_map.67 = (f32[2,64,256]{2,1,0:T(8,128)S(1)}, f32[2,64,256]{2,1,0:T(8,128)S(1)}, f32[2,64,256]{2,1,0:T(8,128)S(1)}) custom-call(f32[2,64,256]{2,1,0:T(8,128)} %bitcast.7, f32[2,64,256]{2,1,0:T(8,128)} %bitcast.8, f32[2,64,256]{2,1,0:T(8,128)} %bitcast.9, f32[2,64,256]{2,1,0:T(8,128)} %bitcast.10), custom_call_target="tpu_custom_call" | custom-call | tf_op jit(solution)/shard_map/pallas_call | solution.py:426
  25.1 0.8 %shard_map.68 = (f32[2,64,256]{2,1,0:T(8,128)}, f32[2,64,256]{2,1,0:T(8,128)}, f32[2,64,256]{2,1,0:T(8,128)}) custom-call(f32[2,64,256]{2,1,0:T(8,128)S(1)} %get-tuple-element.9.refs_0_, f32[2,64,256]{2,1,0:T(8,128)S(1)} %get-tuple-element.10.refs_1_, f32[2,64,256]{2,1,0:T(8,128)S(1)} %get-tuple-element.11.refs_2_), custom_call_target="tpu_custom_call" | custom-call | tf_op jit(solution)/shard_map/pallas_call | solution.py:453
